TPU v7x, 128 devices: a whole 4x4x4 slice. The times are simulated.
128 devices in a mesh: guide: 2 (over core), tensor: 16 (over y, x), batch: 4 (over z).
Axes of the slice: x: 4, y: 4, z: 4, core: 2. Of those that a mesh axis runs over, the one named last changes fastest.
Arguments:
- stream: bfloat16 [2, 512, 2048], P('guide', ('batch', 'tensor')), may hold values from -6 to 6
- attn_gain: float32 [2048], replicated, may hold values from 0.25 to 1.75
- w_qkv: bfloat16 [2048, 3072], P(None, 'tensor'), may hold values from -0.125 to 0.125
- cache_keys: bfloat16 [2, 512, 1024, 512], P('guide', ('batch', 'tensor')), may hold values from -600 to 600
- cache_values: bfloat16 [2, 512, 1024, 512], P('guide', ('batch', 'tensor')), may hold values from -6 to 6
- cache_len: int32 [2, 512], P('guide', ('batch', 'tensor')), may hold values from 1 to 1024, as said below
- w_out: bfloat16 [2048, 2048], P('tensor'), may hold values from -0.125 to 0.125
- mlp_gain: float32 [2048], replicated, may hold values from 0.25 to 1.75
- w_gate: bfloat16 [2048, 8192], P(None, 'tensor'), may hold values from -0.125 to 0.125
- w_up: bfloat16 [2048, 8192], P(None, 'tensor'), may hold values from -0.125 to 0.125
- w_down: bfloat16 [8192, 2048], P('tensor'), may hold values from -0.0625 to 0.0625
- final_gain: float32 [2048], replicated, may hold values from 0.25 to 1.75
- lm_head: bfloat16 [65536, 2048], P(('guide', 'tensor')), may hold values from -128 to 128
- next_gain: float32 [2048], replicated, may hold values from 0.25 to 1.75
- w_next: bfloat16 [2048, 3072], P(None, 'tensor'), may hold values from -0.125 to 0.125
- tenant_counts: int32 [4], replicated, may hold values from 1 to 256, 512 in all
- guide_level: int32 [4], replicated, may hold values from 4 to 16
Outputs:
- logprobs: float32 [512, 65536], P('batch', ('guide', 'tensor'))
- layer_out: bfloat16 [2, 512, 2048], P('guide', ('batch', 'tensor'))
- next_qkv: bfloat16 [2, 512, 3072], P('guide', 'batch', 'tensor')
Inputs may be any that keep to these rules, and one draw needn't show every extreme that they name: `cache_len`: in each branch some request has 1024 cached tokens.
All inputs are finite; a program needn't handle non-finite values.
Results may differ from a plain program's by a relative error of at most 0.024.
Values may be sent and summed in bfloat16 or wider, within the bound.
A program may use at most 128 MiB of HBM per device.

v0:
```python
import math
import jax
import jax.numpy as jnp
from jax import lax
from jax.sharding import PartitionSpec as P

D = 2048
HEADS = 32
KV_HEADS = 8
HEAD_DIM = 64
TENANTS = 4
EPSILON = 1e-05
ROPE_BASE = 500000.0
MASKED = -1e30


def from_partner(block, axis, bit):
    count = lax.axis_size(axis)
    route = []
    for low in range(count):
        high = low | 1 << bit
        if high != low and high < count:
            route += [(low, high), (high, low)]
    return lax.ppermute(block, axis, route)


def rms_norm(values, gain):
    widened = values.astype(jnp.float32)
    factor = lax.rsqrt(jnp.mean(widened * widened, axis=-1, keepdims=True) + EPSILON)
    return (widened * factor * gain).astype(jnp.bfloat16)


def scaled_freq(head_size):
    half_dim = head_size // 2
    steps_up = jnp.arange(half_dim, dtype=jnp.float32)
    base_freq = jnp.exp(steps_up * (-2.0 * math.log(ROPE_BASE) / head_size))
    wavelen = 2.0 * math.pi / base_freq
    smooth = (8192.0 / wavelen - 1.0) / 3.0
    middle = (1.0 - smooth) * base_freq / 32.0 + smooth * base_freq
    return jnp.where(
        wavelen < 2048.0, base_freq, jnp.where(wavelen > 8192.0, base_freq / 32.0, middle)
    )


def rotate(values, position):
    half_dim = values.shape[-1] // 2
    freq = scaled_freq(values.shape[-1])
    angle = position * freq
    cosine = jnp.cos(angle)
    sine = jnp.sin(angle)
    first = values[..., :half_dim].astype(jnp.float32)
    second = values[..., half_dim:].astype(jnp.float32)
    joined = jnp.concatenate(
        [first * cosine - second * sine, second * cosine + first * sine], axis=-1
    )
    return joined.astype(jnp.bfloat16)


def swiglu(normed, w_gate, w_up):
    gate = jnp.dot(normed, w_gate, preferred_element_type=jnp.float32)
    upward = jnp.dot(normed, w_up, preferred_element_type=jnp.float32)
    return (jax.nn.silu(gate) * upward).astype(jnp.bfloat16)


def attend(request_side, keys, values, lengths):
    count = request_side.shape[0]
    kv_width = KV_HEADS * HEAD_DIM
    per_group = HEADS // KV_HEADS
    scale = HEAD_DIM ** (-0.5)
    slot_count = keys.shape[1]
    position = lengths.astype(jnp.float32)[:, None, None]
    queries = rotate(request_side[:, :D].reshape(count, HEADS, HEAD_DIM), position)
    queries = queries.reshape(count, KV_HEADS, per_group, HEAD_DIM)
    new_keys = rotate(
        request_side[:, D : D + kv_width].reshape(count, KV_HEADS, HEAD_DIM), position
    )
    new_values = request_side[:, D + kv_width :].reshape(count, KV_HEADS, HEAD_DIM)
    keys_split = keys.reshape(count, slot_count, KV_HEADS, HEAD_DIM)
    values_split = values.reshape(count, slot_count, KV_HEADS, HEAD_DIM)
    fresh = (
        jnp.einsum("rkgd,rkd->rkg", queries, new_keys, preferred_element_type=jnp.float32) * scale
    )
    slots = jnp.arange(slot_count, dtype=jnp.int32)
    live_mask = (slots[None, :] < lengths[:, None])[:, None, None, :]
    scores = (
        jnp.einsum("rkgd,rlkd->rkgl", queries, keys_split, preferred_element_type=jnp.float32)
        * scale
    )
    scores = jnp.where(live_mask, scores, MASKED)
    peak = jnp.maximum(jnp.max(scores, axis=-1), fresh)
    expd = jnp.where(live_mask, jnp.exp(scores - peak[..., None]), 0.0)
    total = jnp.sum(expd, axis=-1)
    weighted = jnp.einsum(
        "rkgl,rlkd->rkgd",
        expd.astype(jnp.bfloat16),
        values_split,
        preferred_element_type=jnp.float32,
    )
    fresh_exp = jnp.exp(fresh - peak)
    total = total + fresh_exp
    fresh_prob = fresh_exp.astype(jnp.bfloat16).astype(jnp.float32)
    weighted = weighted + fresh_prob[..., None] * new_values.astype(jnp.float32)[:, :, None, :]
    return (weighted / total[..., None]).reshape(count, D).astype(jnp.bfloat16)


def local(
    stream,
    attn_gain,
    w_qkv,
    cache_keys,
    cache_values,
    cache_len,
    w_out,
    mlp_gain,
    w_gate,
    w_up,
    w_down,
    final_gain,
    lm_head,
    next_gain,
    w_next,
    tenant_counts,
    guide_level,
):
    own_rows = stream[0]
    projected = jnp.dot(
        lax.all_gather(rms_norm(own_rows, attn_gain), "tensor", axis=0, tiled=True),
        w_qkv,
        preferred_element_type=jnp.float32,
    ).astype(jnp.bfloat16)
    request_side = lax.all_to_all(projected, "tensor", split_axis=0, concat_axis=1, tiled=True)
    mixed = attend(request_side, cache_keys[0], cache_values[0], cache_len[0])
    head_side = lax.all_to_all(mixed, "tensor", split_axis=1, concat_axis=0, tiled=True)
    selected = head_side
    attn_share = lax.psum_scatter(
        jnp.dot(selected, w_out, preferred_element_type=jnp.float32).astype(jnp.bfloat16),
        "tensor",
        scatter_dimension=0,
        tiled=True,
    ).astype(jnp.float32)
    after_attn = (own_rows.astype(jnp.float32) + attn_share).astype(jnp.bfloat16)
    hidden = swiglu(
        lax.all_gather(rms_norm(after_attn, mlp_gain), "tensor", axis=0, tiled=True), w_gate, w_up
    )
    selected = hidden
    mlp_share = lax.psum_scatter(
        jnp.dot(selected, w_down, preferred_element_type=jnp.float32).astype(jnp.bfloat16),
        "tensor",
        scatter_dimension=0,
        tiled=True,
    ).astype(jnp.float32)
    layer_rows = (after_attn.astype(jnp.float32) + mlp_share).astype(jnp.bfloat16)
    all_out = lax.all_gather(layer_rows, "tensor", axis=0, tiled=True)
    next_rows = jnp.dot(
        rms_norm(all_out, next_gain), w_next, preferred_element_type=jnp.float32
    ).astype(jnp.bfloat16)
    final = rms_norm(all_out, final_gain)
    partner = from_partner(final, "guide", 0)
    is_cond = lax.axis_index("guide") == 0
    cond_rows = jnp.where(is_cond, final, partner)
    uncond_rows = jnp.where(is_cond, partner, final)
    batch_rows = final.shape[0]
    logits = lax.dot_general(
        jnp.concatenate([cond_rows, uncond_rows], axis=0),
        lm_head,
        (((1,), (1,)), ((), ())),
        preferred_element_type=jnp.float32,
    )
    cond_logits = logits[:batch_rows]
    uncond_logits = logits[batch_rows:]
    bounds = jnp.cumsum(tenant_counts)[:-1]
    request_ids = lax.axis_index("batch") * batch_rows + jnp.arange(batch_rows, dtype=jnp.int32)
    tenant = jnp.sum((request_ids[:, None] >= bounds[None, :]).astype(jnp.int32), axis=1)
    chosen = (tenant[:, None] == jnp.arange(TENANTS, dtype=jnp.int32)[None, :]).astype(jnp.float32)
    weight = jnp.sum(chosen * guide_level.astype(jnp.float32)[None, :], axis=1) * 0.25
    guided = uncond_logits + weight[:, None] * (cond_logits - uncond_logits)
    peak = lax.pmax(jnp.max(guided, axis=1), ("guide", "tensor"))
    mass = lax.psum(jnp.sum(jnp.exp(guided - peak[:, None]), axis=1), ("guide", "tensor"))
    logprobs = guided - peak[:, None] - jnp.log(mass)[:, None]
    return (logprobs, layer_rows[None], next_rows[None])


def solution(mesh):
    in_specs = (
        P("guide", ("batch", "tensor"), None),
        P(),
        P(None, "tensor"),
        P("guide", ("batch", "tensor"), None, None),
        P("guide", ("batch", "tensor"), None, None),
        P("guide", ("batch", "tensor")),
        P("tensor", None),
        P(),
        P(None, "tensor"),
        P(None, "tensor"),
        P("tensor", None),
        P(),
        P(("guide", "tensor"), None),
        P(),
        P(None, "tensor"),
        P(),
        P(),
    )
    out_specs = (
        P("batch", ("guide", "tensor")),
        P("guide", ("batch", "tensor"), None),
        P("guide", "batch", "tensor"),
    )
    return jax.shard_map(local, mesh=mesh, in_specs=in_specs, out_specs=out_specs, check_vma=False)
```

profile of v0, /device:TPU:1, one launch (start us, length us, event | category | flops | bytes accessed | tf_op | source)
XLA Modules:
  0.0 462.2 jit_solution(6862168536438569131)
XLA Ops:
  7.2 1.0 fusion.39
  8.2 0.8 fusion.41
  9.1 20.0 %all_gather.9 = bf16[128,2048]{1,0:T(8,128)(2,1)S(1)} all-gather(bf16[8,2048]{1,0:T(8,128)(2,1)S(1)} %fusion.41), channel_id=1, replica_groups=mesh['guide'=2,'tensor'=16,'batch'=4] {'tensor'}, dimensions={0}, use_global_device_ids=true | all-gather | bytes 557056 | tf_op jit(solution)/shard_map/all_gather | solution.py:127
  29.0 1.5 convolution_convert_fusion.3
  30.5 0.7 copy.32
  31.3 4.7 %all-to-all-start = ((bf16[16,8,192]{2,1,0:T(8,128)(2,1)}), bf16[16,8,192]{2,1,0:T(8,128)(2,1)S(1)}, u32[]{:S(2)}, u32[]{:S(2)}) async-start(bf16[16,8,192]{2,1,0:T(8,128)(2,1)} %bitcast.3), calls=%async_computation | async-start | bytes 131072 | tf_op jit(solution)/shard_map/all_to_all | solution.py:131
  36.3 11.4 %copy.34 = bf16[1,8,1024,512]{2,3,1,0:T(8,128)(2,1)} copy(bf16[1,8,1024,512]{3,2,1,0:T(8,128)(2,1)} %param.20) | data formatting | bytes 16777216 | tf_op args[3]
  47.7 11.5 %copy.35 = bf16[1,8,1024,512]{2,3,1,0:T(8,128)(2,1)} copy(bf16[1,8,1024,512]{3,2,1,0:T(8,128)(2,1)} %param.21) | data formatting | bytes 16777216 | tf_op args[4]
  59.8 0.3 fusion.48
  60.1 4.8 %fusion.57 = (f32[8,8,4]{2,1,0:T(8,128)S(1)}, f32[8,8,4,1024]{3,2,1,0:T(4,128)S(1)}) fusion(bf16[8,1024,8,64]{1,3,2,0:T(8,128)(2,1)} %bitcast.42, bf16[8,8,4,32]{3,2,1,0:T(4,128)(2,1)S(1)} %bitcast.47, bf16[8,8,4,32]{3,2,1,0:T(4,128)(2,1)S(1)} %bitcast.45, pred[8,1024]{1,0:T(8,128)(4,1)S(1)} %iota_compare_fusion), kind=kOutput, calls=%fused_computation.103 | convolution fusion | flops 34406144 | bytes 9479168 | tf_op jit(solution)/shard_map/rkgd,rlkd->rkgl/dot_general | solution.py:86
  64.8 0.6 fusion.16
  65.6 5.8 %fusion.5 = bf16[8,8,4,64]{3,2,1,0:T(4,128)(2,1)S(1)} fusion(bf16[8,1024,8,64]{1,3,2,0:T(8,128)(2,1)} %bitcast.43, f32[8,8,4,1024]{3,2,1,0:T(4,128)S(1)} %get-tuple-element.20, f32[8,8,4]{2,1,0:T(8,128)S(1)} %multiply_maximum_fusion, pred[8,1024]{1,0:T(8,128)(4,1)S(1)} %iota_compare_fusion, f32[8,8,4]{2,1,0:T(8,128)S(1)} %get-tuple-element.12, ...), kind=kOutput, calls=%fused_computation.12 | convolution fusion | flops 34406400 | bytes 9497600 | tf_op jit(solution)/shard_map/rkgl,rlkd->rkgd/dot_general | solution.py:93
  71.5 12.9 %all_to_all.35 = bf16[8,16,128]{2,0,1:T(8,128)(2,1)S(1)} all-to-all(bf16[8,16,128]{2,0,1:T(8,128)(2,1)S(1)} %copy.36), channel_id=1, replica_groups=mesh['guide'=2,'tensor'=16,'batch'=4] {'tensor'}, dimensions={1} | all-to-all | bytes 65536 | tf_op jit(solution)/shard_map/all_to_all | solution.py:133
  84.4 2.1 convolution_convert_fusion.1
  86.6 0.6 dynamic-slice
  87.8 88.3 %all-reduce.5.cloned.1.call-done = bf16[128,2048]{1,0:T(8,128)(2,1)} async-done(((bf16[128,2048]{1,0:T(8,128)(2,1)}), bf16[128,2048]{1,0:T(8,128)(2,1)}) %all-reduce.5.cloned.1.call-update) | async-done | bytes 524304
  176.1 0.9 fusion.35
  177.1 17.4 %all_gather.10 = bf16[128,2048]{1,0:T(8,128)(2,1)S(1)} all-gather(bf16[8,2048]{1,0:T(8,128)(2,1)S(1)} %fusion.37), channel_id=1, replica_groups=mesh['guide'=2,'tensor'=16,'batch'=4] {'tensor'}, dimensions={0}, use_global_device_ids=true | all-gather | bytes 557056 | tf_op jit(solution)/shard_map/all_gather | solution.py:143
  194.5 2.0 fusion.58
  196.6 3.2 convolution_convert_fusion
  200.2 89.2 %all-reduce.7.cloned.1.call-done = bf16[128,2048]{1,0:T(8,128)(2,1)} async-done(((bf16[128,2048]{1,0:T(8,128)(2,1)}), bf16[128,2048]{1,0:T(8,128)(2,1)}) %all-reduce.7.cloned.1.call-update) | async-done | bytes 524304
  289.3 0.8 fusion.38
  290.1 17.4 %all_gather.11 = bf16[128,2048]{1,0:T(8,128)(2,1)S(1)} all-gather(bf16[8,2048]{1,0:T(8,128)(2,1)S(1)} %fusion.38), channel_id=1, replica_groups=mesh['guide'=2,'tensor'=16,'batch'=4] {'tensor'}, dimensions={0}, use_global_device_ids=true | all-gather | bytes 557056 | tf_op jit(solution)/shard_map/all_gather | solution.py:153
  307.9 8.1 %collective-permute-start = (bf16[128,2048]{1,0:T(8,128)(2,1)S(1)}, bf16[128,2048]{1,0:T(8,128)(2,1)}, u32[]{:S(2)}, u32[]{:S(2)}) collective-permute-start(bf16[128,2048]{1,0:T(8,128)(2,1)S(1)} %fusion.7), channel_id=1, source_target_pairs={{0,64},{64,0},{1,65},{65,1},{2,66},{66,2},{3,67},{67,3},{4,68},{68... | collective-permute-start | bytes 1572872 | tf_op jit(solution)/shard_map/ppermute | solution.py:24
  316.1 2.2 fusion.6
  318.4 1.4 broadcast_select_fusion.1
  319.8 5.7 %fusion.12 = f32[256,2048]{1,0:T(8,128)S(1)} fusion(bf16[2048,2048]{1,0:T(8,128)(2,1)} %param.29, bf16[128,2048]{1,0:T(8,128)(2,1)S(1)} %get-tuple-element.8, bf16[128,2048]{1,0:T(8,128)(2,1)S(1)} %get-tuple-element.7), kind=kOutput, calls=%fused_computation.22 | convolution fusion | flops 2149580800 | bytes 11534336 | tf_op jit(solution)/shard_map/dot_general | solution.py:163
  325.5 0.4 fusion.54
  326.0 65.0 %pmax.7 = f32[128]{0:T(128)S(1)} all-reduce(f32[128]{0:T(128)S(1)} %get-tuple-element.3), channel_id=1, replica_groups=mesh['guide'=2,'tensor'=16,'batch'=4] {'guide','tensor'}, use_global_device_ids=true, to_apply=%region_11.12 | all-reduce | flops 128 | bytes 1024 | tf_op jit(solution)/shard_map/pmax | solution.py:177
  391.0 0.3 exponential_reduce_fusion
  391.3 62.9 %psum.7 = f32[128]{0:T(128)S(1)} all-reduce(f32[128]{0:T(128)S(1)} %exponential_reduce_fusion), channel_id=1, replica_groups=mesh['guide'=2,'tensor'=16,'batch'=4] {'guide','tensor'}, use_global_device_ids=true, to_apply=%region_13.14 | all-reduce | flops 128 | bytes 1024 | tf_op jit(solution)/shard_map/psum | solution.py:178
  454.2 1.1 subtract_subtract_fusion
  (58 shorter events, 2.1 us)
Async XLA Ops:
  7.2 189.4 %copy-start = (bf16[512,2048]{1,0:T(8,128)(2,1)S(1)}, bf16[512,2048]{1,0:T(8,128)(2,1)}, u32[]{:S(2)}) copy-start(bf16[512,2048]{1,0:T(8,128)(2,1)} %param.27) | copy-start | bytes 6291460
  7.2 28.9 %copy-start.5 = (s32[1,8]{1,0:T(1,128)S(1)}, s32[1,8]{1,0:T(1,128)}, u32[]{:S(2)}) copy-start(s32[1,8]{1,0:T(1,128)} %param.22) | copy-start | bytes 100
  31.3 27.9 %all-to-all-start = ((bf16[16,8,192]{2,1,0:T(8,128)(2,1)}), bf16[16,8,192]{2,1,0:T(8,128)(2,1)S(1)}, u32[]{:S(2)}, u32[]{:S(2)}) async-start(bf16[16,8,192]{2,1,0:T(8,128)(2,1)} %bitcast.3), calls=%async_computation | async-start | bytes 131072 | tf_op jit(solution)/shard_map/all_to_all | solution.py:131
  36.0 140.2 %all-reduce.5.cloned.1.call-start = ((), (), s32[]{:S(2)}) async-start(), calls=%async_computation.2 | async-start | bytes 1048576
  65.5 21.1 %copy-start.9 = (u32[128]{0:T(128)S(1)}, u32[128]{0:T(128)}, u32[]{:S(2)}) copy-start(u32[128]{0:T(128)} %constant.67) | copy-start | bytes 1540
  65.5 110.6 %copy-start.1 = (bf16[1,8,2048]{2,1,0:T(8,128)(2,1)S(1)}, bf16[1,8,2048]{2,1,0:T(8,128)(2,1)}, u32[]{:S(2)}) copy-start(bf16[1,8,2048]{2,1,0:T(8,128)(2,1)} %param.17) | copy-start | bytes 98308
  65.6 111.5 %copy-start.4 = (f32[2048]{0:T(1024)S(1)}, f32[2048]{0:T(1024)}, u32[]{:S(2)}) copy-start(f32[2048]{0:T(1024)} %param.24) | copy-start | bytes 24580
  86.5 202.8 %all-reduce.7.cloned.1.call-start = ((), (), s32[]{:S(2)}) async-start(), calls=%async_computation.3 | async-start | bytes 1048576
  196.6 3.3 copy-start.7
  196.6 111.1 %copy-start.3 = (f32[2048]{0:T(1024)S(1)}, f32[2048]{0:T(1024)}, u32[]{:S(2)}) copy-start(f32[2048]{0:T(1024)} %param.28) | copy-start | bytes 24580
  199.8 116.2 %copy-start.8 = (s32[4]{0:T(128)S(1)}, s32[4]{0:T(128)}, u32[]{:S(2)}) copy-start(s32[4]{0:T(128)} %param.33) | copy-start | bytes 52
  199.8 116.3 %copy-start.6 = (f32[2048]{0:T(1024)S(1)}, f32[2048]{0:T(1024)}, u32[]{:S(2)}) copy-start(f32[2048]{0:T(1024)} %param.30) | copy-start | bytes 24580
  290.1 29.7 %copy-start.2 = (bf16[8,2048]{1,0:T(8,128)(2,1)}, bf16[8,2048]{1,0:T(8,128)(2,1)S(1)}, u32[]{:S(2)}) copy-start(bf16[8,2048]{1,0:T(8,128)(2,1)S(1)} %fusion.38) | copy-start | bytes 98308
  307.9 10.4 %collective-permute-start = (bf16[128,2048]{1,0:T(8,128)(2,1)S(1)}, bf16[128,2048]{1,0:T(8,128)(2,1)}, u32[]{:S(2)}, u32[]{:S(2)}) collective-permute-start(bf16[128,2048]{1,0:T(8,128)(2,1)S(1)} %fusion.7), channel_id=1, source_target_pairs={{0,64},{64,0},{1,65},{65,1},{2,66},{66,2},{3,67},{67,3},{4,68},{68... | collective-permute-start | bytes 1572872 | tf_op jit(solution)/shard_map/ppermute | solution.py:24
Sparse Core Ops, SparseCore 0:
  86.7 89.4 all-reduce.4
  200.0 89.2 all-reduce.6
where the time goes:
time: 464 us; the launch traced here: 462 us
  blocking collectives  196 us (42%)
  waiting for transfers between devices  178 us (38%)
  matrix products  27.7 us (6%)
  local copies, waits for them, and re-layouts  24.8 us (5%)
  between operations  14.9 us (3%)
  starting transfers between devices  12.9 us (3%)
  other arithmetic  8.77 us (2%)
    unnamed x4, waiting for transfers between devices  177 us
    pmax x1, blocking collectives, local(): peak = lax.pmax(jnp.max(guided, axis=1), ('guide', 'tensor'))  65 us
    psum x1, blocking collectives, local(): lax.psum(jnp.sum(jnp.exp(guided - peak[:, None]), axis=1), ('guide', 'ten...  62.9 us
    unnamed x23, local copies, waits for them, and re-layouts  23.5 us
    all_gather x1, blocking collectives, local(): lax.all_gather(rms_norm(own_rows, attn_gain), 'tensor', axis=0, tiled=True)  20 us
    all_gather x1, blocking collectives, local(): all_out = lax.all_gather(layer_rows, 'tensor', axis=0, tiled=True)  17.4 us
    all_gather x1, blocking collectives, local(): lax.all_gather(rms_norm(after_attn, mlp_gain), 'tensor', axis=0, tiled=True)  17.4 us
    all_to_all x1, blocking collectives, local(): lax.all_to_all(mixed, 'tensor', split_axis=1, concat_axis=0, tiled=True)  12.9 us
  transfers between devices with their start and end apart: 4, of which 2 were waited for; matrix products, arithmetic and copies ran while one was open for 6% of the time, Pallas kernels for 0%

commit v1 on v0

--- a/solution.py
+++ b/solution.py
@@ -150,7 +150,9 @@
         tiled=True,
     ).astype(jnp.float32)
     layer_rows = (after_attn.astype(jnp.float32) + mlp_share).astype(jnp.bfloat16)
-    all_out = lax.all_gather(layer_rows, "tensor", axis=0, tiled=True)
+    all_out = jnp.concatenate(
+        lax.all_to_all(jnp.stack([layer_rows] * lax.axis_size("tensor")), "tensor", 0, 0), axis=0
+    )
     next_rows = jnp.dot(
         rms_norm(all_out, next_gain), w_next, preferred_element_type=jnp.float32
     ).astype(jnp.bfloat16)

time: 464 us -> 456 us (0.983)
  blocking collectives: 196 us -> 178 us
  waiting for transfers between devices: 178 us -> 187 us
    all_gather x1 -> x0, blocking collectives: 17.4 us -> none  [local(): all_out = lax.all_gather(layer_rows, 'tensor', axis=0, tiled=True)]
    all_to_all x0 -> x1, waiting for transfers between devices: none -> 8.71 us  [local(): lax.all_to_all(jnp.stack([layer_rows] * lax.axis_size('tensor')), 'tensor...]
  transfers between devices with their start and end apart: 4 -> 5, of which waited for: 2 -> 3; matrix products, arithmetic and copies ran while one was open for 6% -> 6% of each run, Pallas kernels for 0% -> 0%
where the time goes in v1:
time: 456 us; the launch traced here: 455 us
  waiting for transfers between devices  187 us (41%)
  blocking collectives  178 us (39%)
  matrix products  27.6 us (6%)
  local copies, waits for them, and re-layouts  25.8 us (6%)
  between operations  14.9 us (3%)
  starting transfers between devices  13.1 us (3%)
  other arithmetic  8.77 us (2%)
    unnamed x4, waiting for transfers between devices  178 us
    psum x1, blocking collectives, local(): lax.psum(jnp.sum(jnp.exp(guided - peak[:, None]), axis=1), ('guide', 'ten...  64.5 us
    pmax x1, blocking collectives, local(): peak = lax.pmax(jnp.max(guided, axis=1), ('guide', 'tensor'))  63.5 us
    unnamed x23, local copies, waits for them, and re-layouts  23.5 us
    all_gather x1, blocking collectives, local(): lax.all_gather(rms_norm(own_rows, attn_gain), 'tensor', axis=0, tiled=True)  20 us
    all_gather x1, blocking collectives, local(): lax.all_gather(rms_norm(after_attn, mlp_gain), 'tensor', axis=0, tiled=True)  17.4 us
    all_to_all x1, blocking collectives, local(): lax.all_to_all(mixed, 'tensor', split_axis=1, concat_axis=0, tiled=True)  12.9 us
  transfers between devices with their start and end apart: 5, of which 3 were waited for; matrix products, arithmetic and copies ran while one was open for 6% of the time, Pallas kernels for 0%

profile of v1, /device:TPU:1, one launch (start us, length us, event | category | flops | bytes accessed | tf_op | source)
XLA Modules:
  0.0 455.0 jit_solution(14989265230573051497)
XLA Ops:
  7.2 1.0 fusion.40
  8.2 0.8 fusion.42
  9.1 20.0 %all_gather.6 = bf16[128,2048]{1,0:T(8,128)(2,1)S(1)} all-gather(bf16[8,2048]{1,0:T(8,128)(2,1)S(1)} %fusion.42), channel_id=1, replica_groups=mesh['guide'=2,'tensor'=16,'batch'=4] {'tensor'}, dimensions={0}, use_global_device_ids=true | all-gather | bytes 557056 | tf_op jit(solution)/shard_map/all_gather | solution.py:127
  29.0 1.5 convolution_convert_fusion.3
  30.5 0.7 copy.32
  31.3 4.7 %all-to-all-start = ((bf16[16,8,192]{2,1,0:T(8,128)(2,1)}), bf16[16,8,192]{2,1,0:T(8,128)(2,1)S(1)}, u32[]{:S(2)}, u32[]{:S(2)}) async-start(bf16[16,8,192]{2,1,0:T(8,128)(2,1)} %bitcast.3), calls=%async_computation | async-start | bytes 131072 | tf_op jit(solution)/shard_map/all_to_all | solution.py:131
  36.3 11.4 %copy.34 = bf16[1,8,1024,512]{2,3,1,0:T(8,128)(2,1)} copy(bf16[1,8,1024,512]{3,2,1,0:T(8,128)(2,1)} %param.20) | data formatting | bytes 16777216 | tf_op args[3]
  47.7 11.5 %copy.35 = bf16[1,8,1024,512]{2,3,1,0:T(8,128)(2,1)} copy(bf16[1,8,1024,512]{3,2,1,0:T(8,128)(2,1)} %param.21) | data formatting | bytes 16777216 | tf_op args[4]
  60.1 4.8 %fusion.58 = (f32[8,8,4]{2,1,0:T(8,128)S(1)}, f32[8,8,4,1024]{3,2,1,0:T(4,128)S(1)}) fusion(bf16[8,1024,8,64]{1,3,2,0:T(8,128)(2,1)} %bitcast.57, bf16[8,8,4,32]{3,2,1,0:T(4,128)(2,1)S(1)} %bitcast.62, bf16[8,8,4,32]{3,2,1,0:T(4,128)(2,1)S(1)} %bitcast.60, pred[8,1024]{1,0:T(8,128)(4,1)S(1)} %iota_compare_fusion), kind=kOutput, calls=%fused_computation.104 | convolution fusion | flops 34406144 | bytes 9479168 | tf_op jit(solution)/shard_map/rkgd,rlkd->rkgl/dot_general | solution.py:86
  64.8 0.6 fusion.17
  65.6 5.8 %fusion.3 = bf16[8,8,4,64]{3,2,1,0:T(4,128)(2,1)S(1)} fusion(bf16[8,1024,8,64]{1,3,2,0:T(8,128)(2,1)} %bitcast.58, f32[8,8,4,1024]{3,2,1,0:T(4,128)S(1)} %get-tuple-element.20, f32[8,8,4]{2,1,0:T(8,128)S(1)} %multiply_maximum_fusion, pred[8,1024]{1,0:T(8,128)(4,1)S(1)} %iota_compare_fusion, f32[8,8,4]{2,1,0:T(8,128)S(1)} %get-tuple-element.12, ...), kind=kOutput, calls=%fused_computation.10 | convolution fusion | flops 34406400 | bytes 9497600 | tf_op jit(solution)/shard_map/rkgl,rlkd->rkgd/dot_general | solution.py:93
  71.5 12.9 %all_to_all.40 = bf16[8,16,128]{2,0,1:T(8,128)(2,1)S(1)} all-to-all(bf16[8,16,128]{2,0,1:T(8,128)(2,1)S(1)} %copy.36), channel_id=1, replica_groups=mesh['guide'=2,'tensor'=16,'batch'=4] {'tensor'}, dimensions={1} | all-to-all | bytes 65536 | tf_op jit(solution)/shard_map/all_to_all | solution.py:133
  84.4 2.1 convolution_convert_fusion.1
  86.6 0.6 dynamic-slice
  87.8 88.3 %all-reduce.5.cloned.1.call-done = bf16[128,2048]{1,0:T(8,128)(2,1)} async-done(((bf16[128,2048]{1,0:T(8,128)(2,1)}), bf16[128,2048]{1,0:T(8,128)(2,1)}) %all-reduce.5.cloned.1.call-update) | async-done | bytes 524304
  176.1 0.9 fusion.36
  177.1 17.4 %all_gather.7 = bf16[128,2048]{1,0:T(8,128)(2,1)S(1)} all-gather(bf16[8,2048]{1,0:T(8,128)(2,1)S(1)} %fusion.38), channel_id=1, replica_groups=mesh['guide'=2,'tensor'=16,'batch'=4] {'tensor'}, dimensions={0}, use_global_device_ids=true | all-gather | bytes 557056 | tf_op jit(solution)/shard_map/all_gather | solution.py:143
  194.5 2.0 fusion.59
  196.6 3.2 convolution_convert_fusion
  199.8 89.5 %all-reduce.7.cloned.1.call-done = bf16[128,2048]{1,0:T(8,128)(2,1)} async-done(((bf16[128,2048]{1,0:T(8,128)(2,1)}), bf16[128,2048]{1,0:T(8,128)(2,1)}) %all-reduce.7.cloned.1.call-update) | async-done | bytes 524304
  289.3 0.8 fusion.39
  290.1 0.8 stack.4
  291.0 4.1 all-to-all-start.2
  295.3 8.7 %all-to-all-done.2 = bf16[16,8,2048]{2,1,0:T(8,128)(2,1)S(1)} async-done(((bf16[16,8,2048]{2,1,0:T(8,128)(2,1)}), bf16[16,8,2048]{2,1,0:T(8,128)(2,1)S(1)}, u32[]{:S(2)}, u32[]{:S(2)}) %all-to-all-start.2) | async-done | bytes 524320 | tf_op jit(solution)/shard_map/all_to_all | solution.py:154
  304.5 4.2 collective-permute-start
  308.9 2.2 fusion.4
  311.1 1.4 broadcast_select_fusion.1
  312.5 5.7 %fusion.13 = f32[256,2048]{1,0:T(8,128)S(1)} fusion(bf16[2048,2048]{1,0:T(8,128)(2,1)} %param.29, bf16[128,2048]{1,0:T(8,128)(2,1)S(1)} %get-tuple-element.8, bf16[128,2048]{1,0:T(8,128)(2,1)S(1)} %get-tuple-element.7), kind=kOutput, calls=%fused_computation.23 | convolution fusion | flops 2149580800 | bytes 11534336 | tf_op jit(solution)/shard_map/dot_general | solution.py:165
  318.3 0.4 fusion.55
  318.7 63.5 %pmax.7 = f32[128]{0:T(128)S(1)} all-reduce(f32[128]{0:T(128)S(1)} %get-tuple-element.3), channel_id=1, replica_groups=mesh['guide'=2,'tensor'=16,'batch'=4] {'guide','tensor'}, use_global_device_ids=true, to_apply=%region_11.12 | all-reduce | flops 128 | bytes 1024 | tf_op jit(solution)/shard_map/pmax | solution.py:179
  382.5 64.5 %psum.7 = f32[128]{0:T(128)S(1)} all-reduce(f32[128]{0:T(128)S(1)} %exponential_reduce_fusion), channel_id=1, replica_groups=mesh['guide'=2,'tensor'=16,'batch'=4] {'guide','tensor'}, use_global_device_ids=true, to_apply=%region_13.14 | all-reduce | flops 128 | bytes 1024 | tf_op jit(solution)/shard_map/psum | solution.py:180
  447.0 1.1 subtract_subtract_fusion
  (61 shorter events, 2.7 us)
Async XLA Ops:
  7.2 189.4 %copy-start = (bf16[512,2048]{1,0:T(8,128)(2,1)S(1)}, bf16[512,2048]{1,0:T(8,128)(2,1)}, u32[]{:S(2)}) copy-start(bf16[512,2048]{1,0:T(8,128)(2,1)} %param.27) | copy-start | bytes 6291460
  7.2 28.9 %copy-start.5 = (s32[1,8]{1,0:T(1,128)S(1)}, s32[1,8]{1,0:T(1,128)}, u32[]{:S(2)}) copy-start(s32[1,8]{1,0:T(1,128)} %param.22) | copy-start | bytes 100
  31.3 27.9 %all-to-all-start = ((bf16[16,8,192]{2,1,0:T(8,128)(2,1)}), bf16[16,8,192]{2,1,0:T(8,128)(2,1)S(1)}, u32[]{:S(2)}, u32[]{:S(2)}) async-start(bf16[16,8,192]{2,1,0:T(8,128)(2,1)} %bitcast.3), calls=%async_computation | async-start | bytes 131072 | tf_op jit(solution)/shard_map/all_to_all | solution.py:131
  36.0 140.2 %all-reduce.5.cloned.1.call-start = ((), (), s32[]{:S(2)}) async-start(), calls=%async_computation.3 | async-start | bytes 1048576
  65.5 21.1 %copy-start.9 = (u32[128]{0:T(128)S(1)}, u32[128]{0:T(128)}, u32[]{:S(2)}) copy-start(u32[128]{0:T(128)} %constant.67) | copy-start | bytes 1540
  65.5 110.6 %copy-start.1 = (bf16[1,8,2048]{2,1,0:T(8,128)(2,1)S(1)}, bf16[1,8,2048]{2,1,0:T(8,128)(2,1)}, u32[]{:S(2)}) copy-start(bf16[1,8,2048]{2,1,0:T(8,128)(2,1)} %param.17) | copy-start | bytes 98308
  65.6 111.5 %copy-start.4 = (f32[2048]{0:T(1024)S(1)}, f32[2048]{0:T(1024)}, u32[]{:S(2)}) copy-start(f32[2048]{0:T(1024)} %param.24) | copy-start | bytes 24580
  86.5 202.8 %all-reduce.7.cloned.1.call-start = ((), (), s32[]{:S(2)}) async-start(), calls=%async_computation.4 | async-start | bytes 1048576
  199.8 95.3 %copy-start.7 = (s32[4]{0:T(128)S(1)}, s32[4]{0:T(128)}, u32[]{:S(2)}) copy-start(s32[4]{0:T(128)} %param.32) | copy-start | bytes 52
  199.8 104.5 %copy-start.3 = (f32[2048]{0:T(1024)S(1)}, f32[2048]{0:T(1024)}, u32[]{:S(2)}) copy-start(f32[2048]{0:T(1024)} %param.28) | copy-start | bytes 24580
  199.8 109.0 %copy-start.8 = (s32[4]{0:T(128)S(1)}, s32[4]{0:T(128)}, u32[]{:S(2)}) copy-start(s32[4]{0:T(128)} %param.33) | copy-start | bytes 52
  199.8 109.1 %copy-start.6 = (f32[2048]{0:T(1024)S(1)}, f32[2048]{0:T(1024)}, u32[]{:S(2)}) copy-start(f32[2048]{0:T(1024)} %param.30) | copy-start | bytes 24580
  290.1 21.0 %copy-start.2 = (bf16[8,2048]{1,0:T(8,128)(2,1)}, bf16[8,2048]{1,0:T(8,128)(2,1)S(1)}, u32[]{:S(2)}) copy-start(bf16[8,2048]{1,0:T(8,128)(2,1)S(1)} %fusion.39) | copy-start | bytes 98308
  291.0 13.1 %all-to-all-start.2 = ((bf16[16,8,2048]{2,1,0:T(8,128)(2,1)}), bf16[16,8,2048]{2,1,0:T(8,128)(2,1)S(1)}, u32[]{:S(2)}, u32[]{:S(2)}) async-start(bf16[16,8,2048]{2,1,0:T(8,128)(2,1)} %stack.4), calls=%async_computation.2 | async-start | bytes 1048576 | tf_op jit(solution)/shard_map/all_to_all | solution.py:154
  304.5 6.6 %collective-permute-start = (bf16[128,2048]{1,0:T(8,128)(2,1)S(1)}, bf16[128,2048]{1,0:T(8,128)(2,1)}, u32[]{:S(2)}, u32[]{:S(2)}) collective-permute-start(bf16[128,2048]{1,0:T(8,128)(2,1)S(1)} %fusion.8), channel_id=1, source_target_pairs={{0,64},{64,0},{1,65},{65,1},{2,66},{66,2},{3,67},{67,3},{4,68},{68... | collective-permute-start | bytes 1572872 | tf_op jit(solution)/shard_map/ppermute | solution.py:24
Sparse Core Ops, SparseCore 0:
  86.7 89.4 all-reduce.4
  200.0 89.3 all-reduce.6
